TPU v7x, 32 devices: a whole 2x2x4 slice. The times are simulated.
32 devices in a mesh: groups: 2 (over y), expo: 4 (over z), tile: 4 (over x, core).
Axes of the slice: x: 2, y: 2, z: 4, core: 2. Of those that a mesh axis runs over, the one named last changes fastest.
Arguments:
- template: bfloat16 [8, 64, 4096], P(('groups', 'expo'), 'tile'), parts along dimension 0
- science: bfloat16 [8, 1, 64, 4096], P(('groups', 'expo'), None, 'tile'), parts along dimension 0
- plan: int32 [8], P('groups'), parts along dimension 0, may hold values from 0 to 3, as said below
- orders: int32 [6, 2], replicated, may hold values from 0 to 2
- coadd_weight: float32 [8, 1], P(('groups', 'expo')), parts along dimension 0, may hold values from 0.3 to 3
- intersection: int32 [8, 1], P(('groups', 'expo')), parts along dimension 0, may hold values 0 or 1
Outputs:
- coadd: float32 [2, 64, 4096], P('groups', 'tile', 'expo'), parts along dimension 0
- coeffs: float32 [8, 1, 13], P(('groups', 'expo')), parts along dimension 0
There are 2 independent parts, one for each index of `groups`. A program takes and returns all parts, laid end to end along the dimension named above; an argument that names none is the same for every part. Nothing has to cross between parts.
Inputs may be any that keep to these rules, and one draw needn't show every extreme that they name: `plan`: a permutation of the group's patch indices.
All inputs are finite; a program needn't handle non-finite values. No bound on the sum of `intersection` on one device may be relied on, other than what follows from the above.
Results may differ from a plain program's by a relative error of at most 0.0061.
Values may be sent and summed in bfloat16 or wider, within the bound.
A program may use at most 64 MiB of HBM per device.

v0:
```python
import functools

import jax
import jax.numpy as jnp
from jax import lax
from jax.experimental import pallas as pl
from jax.experimental.pallas import tpu as pltpu
from jax.sharding import PartitionSpec as P

HALF = 15
NB = 6
NU = 13


SIGMAS = (0.8, 1.4, 2.2, 3.0, 4.0, 5.5)
RIDGE = 0.05


def broadcast(block, axis, holder):
    block = jnp.where(lax.axis_index(axis) == holder, block, jnp.zeros_like(block))
    return lax.psum(block, axis)


def extended(x, sides, width):
    for axis, dim in sides:
        size, length = (lax.axis_size(axis), x.shape[dim])
        up = [(i, (i + 1) % size) for i in range(size - 1)]
        down = [(j, i) for i, j in up]
        last = lax.slice_in_dim(x, length - width, length, axis=dim)
        first = lax.slice_in_dim(x, 0, width, axis=dim)
        before = lax.ppermute(last, axis, up)
        after = lax.ppermute(first, axis, down)
        x = jnp.concatenate([before, x, after], axis=dim)
    return x


def make_filters(orders):
    taps_pos = jnp.arange(2 * HALF + 1).astype(jnp.float32) - HALF
    row_list = []
    col_list = []
    for basis in range(NB):
        sigma = SIGMAS[basis]
        envelope = jnp.exp(-taps_pos * taps_pos / (2.0 * sigma * sigma))

        def power(order):
            return jnp.where(order == 0, 1.0, jnp.where(order == 1, taps_pos, taps_pos * taps_pos))

        row_filter = envelope * power(orders[basis, 0])
        col_filter = envelope * power(orders[basis, 1])
        row_list.append(row_filter / jnp.sqrt(jnp.sum(row_filter * row_filter)))
        col_list.append(col_filter / jnp.sqrt(jnp.sum(col_filter * col_filter)))
    return (jnp.stack(row_list).astype(jnp.bfloat16), jnp.stack(col_list).astype(jnp.bfloat16))


def band_matrix(filters, out_len, in_len):
    offset = jnp.arange(in_len)[None, :] - jnp.arange(out_len)[:, None]
    taps_idx = jnp.arange(2 * HALF + 1)
    picks = (offset[:, :, None] == taps_idx[None, None, :]).astype(jnp.float32)
    band = jnp.einsum("ijt,kt->kij", picks, filters.astype(jnp.float32))
    return band.astype(jnp.bfloat16)


def per_device(template, science, plan, orders, coadd_weight, intersection):
    row_filters, col_filters = make_filters(orders)
    rows = template.shape[1]
    width = template.shape[2]
    blocks_count = width // 128
    steps_count = science.shape[1]
    row_band = band_matrix(row_filters, rows, rows + 2 * HALF)
    col_band = jnp.transpose(band_matrix(col_filters, 128, 128 + 2 * HALF), (0, 2, 1))
    column_pos = 2.0 * (jnp.arange(width).astype(jnp.float32) + 0.5) / width - 1.0
    pieces = []
    fitted = []
    for step in range(steps_count):
        owner_index = plan[step]
        received = broadcast(template[0], "expo", owner_index)
        padded = extended(received, (("tile", 0),), HALF)
        rowconv = jnp.einsum(
            "kij,jw->kiw", row_band, padded, preferred_element_type=jnp.float32
        ).astype(jnp.bfloat16)
        blocks = rowconv.reshape(NB, rows, blocks_count, 128)
        empty_rim = jnp.zeros((NB, rows, 1, HALF), jnp.bfloat16)
        previous = jnp.concatenate([empty_rim, blocks[:, :, :-1, 128 - HALF :]], axis=2)
        following = jnp.concatenate([blocks[:, :, 1:, :HALF], empty_rim], axis=2)
        window = jnp.concatenate([previous, blocks, following], axis=3)
        conv = jnp.einsum("krbj,kjc->krbc", window, col_band, preferred_element_type=jnp.float32)
        conv = conv.reshape(NB, rows, width)
        fields = jnp.concatenate(
            [conv, conv * column_pos, jnp.ones((1, rows, width), jnp.float32)], axis=0
        )
        fields = fields.reshape(NU, rows * width)
        exposure_image = science[0, step].astype(jnp.float32).reshape(rows * width)
        normal_local = jnp.dot(fields, fields.T, precision=lax.Precision.HIGHEST)
        project_local = jnp.dot(fields, exposure_image, precision=lax.Precision.HIGHEST)
        normal_matrix, projections = lax.psum((normal_local, project_local), "tile")
        normal_matrix = normal_matrix + RIDGE * (jnp.trace(normal_matrix) / NU) * jnp.eye(
            NU, dtype=jnp.float32
        )
        factor = jnp.linalg.cholesky(normal_matrix)
        coeffs = jax.scipy.linalg.cho_solve((factor, True), projections)
        model = jnp.dot(coeffs, fields, precision=lax.Precision.HIGHEST)
        difference = exposure_image - model
        weight_now = coadd_weight[0, step] * intersection[0, step].astype(jnp.float32)
        pieces.append((weight_now * difference).reshape(rows, width))
        fitted.append(coeffs)
    weighted = jnp.stack(pieces)
    received_parts = lax.all_to_all(weighted[None], "expo", split_axis=3, concat_axis=0, tiled=True)
    coadd = jnp.sum(received_parts, axis=0)
    return (coadd, jnp.stack(fitted)[None])


LANES = 128
VMEM_BYTES = 67043328
WIDE = 256
PAIRS = [(u, v) for u in range(NB) for v in range(u + 1)]
MESH = pl.DeviceIdType.MESH


def taps(position, sigma, order):
    power = jnp.where(order == 0, 1.0, jnp.where(order == 1, position, position * position))
    value = jnp.exp(-position * position / (2.0 * sigma * sigma)) * power
    return jnp.where(jnp.abs(position) <= HALF, value, 0.0)


def fused(
    dims,
    template_ref,
    science_ref,
    plan_ref,
    orders_ref,
    weight_ref,
    inter_ref,
    coadd_ref,
    coeffs_ref,
    tbuf,
    sbuf,
    rbuf,
    row_band,
    col_band,
    conv_ref,
    stat_ref,
    local_sem,
    tsend,
    trecv,
    ssend,
    srecv,
    fsend,
    frecv,
    rsend,
    rrecv,
):
    expos, tiles, rows, width, cols = dims
    per = cols // LANES
    span = cols + 2 * LANES
    blocks = cols // WIDE
    chunks = [(b, h) for b in range(blocks) for h in range(WIDE // LANES)]
    me = lax.axis_index("expo")
    tile = lax.axis_index("tile")

    def others():
        for de in range(expos):
            for dt in range(tiles):
                if de or dt:
                    yield de * tiles + dt, (me + de) % expos, (tile + dt) % tiles

    barrier = pltpu.get_barrier_semaphore()
    for d in range(1, expos):
        peer = (me + d) % expos
        pl.semaphore_signal(barrier, inc=1, device_id={"expo": peer}, device_id_type=MESH)
    for d in (1, tiles - 1):
        peer = (tile + d) % tiles
        pl.semaphore_signal(barrier, inc=1, device_id={"tile": peer}, device_id_type=MESH)

    def source_start(e):
        return e * per - 1 + (expos - 1 - e) // (expos - 1) - e // (expos - 1)

    def source_columns(e):
        return pl.ds(pl.multiple_of(source_start(e) * LANES, LANES), span)

    def window_columns(e):
        return pl.ds(pl.multiple_of((source_start(e) - e * per + 2) * LANES, LANES), span)

    def own_columns(e):
        return pl.ds(pl.multiple_of(e * cols, LANES), cols)

    mine = pltpu.make_async_copy(
        template_ref.at[0, :, source_columns(me)],
        tbuf.at[me, 1, :, window_columns(me)],
        local_sem.at[0],
    )
    mine.start()
    mine_science = pltpu.make_async_copy(
        science_ref.at[0, 0, :, own_columns(me)], sbuf.at[me], local_sem.at[1]
    )
    mine_science.start()

    def template_copy(d, target, holder):
        return pltpu.make_async_remote_copy(
            src_ref=template_ref.at[0, :, source_columns(target)],
            dst_ref=tbuf.at[holder, 1, :, window_columns(target)],
            send_sem=tsend.at[d],
            recv_sem=trecv.at[d],
            device_id={"expo": target},
            device_id_type=MESH,
        )

    def science_copy(d, target, holder):
        return pltpu.make_async_remote_copy(
            src_ref=science_ref.at[0, 0, :, own_columns(target)],
            dst_ref=sbuf.at[holder],
            send_sem=ssend.at[d],
            recv_sem=srecv.at[d],
            device_id={"expo": target},
            device_id_type=MESH,
        )

    def forward_copy(d, holder, side):
        target = tile + 1 if side == 0 else tile - 1
        return pltpu.make_async_remote_copy(
            src_ref=tbuf.at[holder, 1, :, window_columns(me)],
            dst_ref=tbuf.at[holder, 2 * side, :, window_columns(me)],
            send_sem=fsend.at[side, d],
            recv_sem=frecv.at[side, d],
            device_id={"tile": target},
            device_id_type=MESH,
        )

    def forward(d, holder):
        @pl.when(tile < tiles - 1)
        def _():
            forward_copy(d, holder, 0).start()

        @pl.when(tile > 0)
        def _():
            forward_copy(d, holder, 1).start()

    position = lax.broadcasted_iota(jnp.int32, (1, LANES), 1).astype(jnp.float32) - HALF
    for k in range(NB):
        sigma = SIGMAS[k]
        for side, length in ((0, rows), (1, LANES)):
            order = jnp.full((1, LANES), orders_ref[side, k], jnp.int32)
            line = taps(position, sigma, order)
            root = jnp.sqrt(jnp.sum(line * line, axis=1, keepdims=True))
            scale = 1.0 / root
            if side == 0:
                shape = (rows, 3 * rows)
                offset = (
                    lax.broadcasted_iota(jnp.int32, shape, 1)
                    - lax.broadcasted_iota(jnp.int32, shape, 0)
                    - rows
                ).astype(jnp.float32)
                band = taps(offset, sigma, jnp.full(shape, orders_ref[side, k], jnp.int32))
                row_band[k * rows : (k + 1) * rows, :] = (band * scale).astype(jnp.bfloat16)
            else:
                shape = (LANES, LANES)
                delta = lax.broadcasted_iota(jnp.int32, shape, 0) - lax.broadcasted_iota(
                    jnp.int32, shape, 1
                )
                column_order = jnp.full(shape, orders_ref[side, k], jnp.int32)
                zero = jnp.zeros(shape, jnp.bfloat16)
                parts = {}
                for kind in range(3):
                    offset = (delta + (kind - 1) * LANES).astype(jnp.float32)
                    band = taps(offset, sigma, column_order)
                    parts[kind] = (band * scale).astype(jnp.bfloat16)
                for jb in range(WIDE // LANES + 2):
                    for cb in range(WIDE // LANES):
                        col_band[
                            k,
                            jb * LANES : (jb + 1) * LANES,
                            cb * LANES : (cb + 1) * LANES,
                        ] = parts.get(jb - cb, zero)

    pl.semaphore_wait(barrier, expos + 1)
    for d in reversed(range(1, expos)):
        template_copy(d, (me + d) % expos, me).start()
    mine.wait()
    forward(0, me)
    for d in range(1, expos):
        science_copy(d, (me + d) % expos, me).start()

    for d in reversed(range(1, expos)):
        holder = (me + expos - d) % expos
        template_copy(d, me, holder).wait_recv()
        forward(d, holder)

    @pl.when(tile > 0)
    def _():
        for d in range(expos):
            forward_copy(d, (me + expos - d) % expos, 0).wait_recv()

    @pl.when(tile < tiles - 1)
    def _():
        for d in range(expos):
            forward_copy(d, (me + expos - d) % expos, 1).wait_recv()

    @pl.when(tile < tiles - 1)
    def _():
        for d in range(expos):
            forward_copy(d, (me + expos - d) % expos, 0).wait_send()

    @pl.when(tile > 0)
    def _():
        for d in range(expos):
            forward_copy(d, (me + expos - d) % expos, 1).wait_send()

    owner = plan_ref[0]
    shape = (rows, span)
    column = lax.broadcasted_iota(jnp.int32, shape, 1) + (me * cols - LANES)
    inside = (column >= 0) & (column < width)
    pieces = []
    for part in range(3):
        block = tbuf[owner, part, :, LANES : LANES + span].astype(jnp.float32)
        keep = inside
        if part == 0:
            keep = keep & (jnp.full(shape, tile, jnp.int32) > 0)
        if part == 2:
            keep = keep & (jnp.full(shape, tile, jnp.int32) < tiles - 1)
        pieces.append(jnp.where(keep, block, 0.0).astype(jnp.bfloat16))
    rows_window = jnp.concatenate(pieces, axis=0)
    rowconv = jnp.dot(
        row_band[...], rows_window, preferred_element_type=jnp.float32
    ).astype(jnp.bfloat16)
    for k in range(NB):
        mine_rows = rowconv[k * rows : (k + 1) * rows]
        windows = jnp.concatenate(
            [mine_rows[:, b * WIDE : (b + 1) * WIDE + 2 * LANES] for b in range(blocks)], axis=0
        )
        conv_ref[k] = jnp.dot(windows, col_band[k], preferred_element_type=jnp.float32)

    def conv_at(k, b, h):
        return conv_ref[k, b * rows : (b + 1) * rows, h * LANES : (h + 1) * LANES]

    def science_at(e, b, h):
        start = b * WIDE + h * LANES
        return sbuf[e, :, start : start + LANES].astype(jnp.float32)

    def fold(x):
        return x.reshape(rows // 8, 8, LANES).sum(axis=0)

    lane = lax.broadcasted_iota(jnp.int32, (1, LANES), 1)
    columns = {}
    for b, h in chunks:
        place = (me * cols + b * WIDE + h * LANES + lane).astype(jnp.float32)
        columns[b, h] = 2.0 * (place + 0.5) / width - 1.0

    def put(index, value):
        stat_ref[index : index + 1, :] = jnp.sum(value, axis=0, keepdims=True)

    count = 3 * len(PAIRS) + 2 * NB
    for index, (u, v) in enumerate(PAIRS):
        sums = [0.0, 0.0, 0.0]
        for b, h in chunks:
            product = fold(conv_at(u, b, h) * conv_at(v, b, h))
            once = product * columns[b, h]
            sums = [sums[0] + product, sums[1] + once, sums[2] + once * columns[b, h]]
        for moment in range(3):
            put(3 * index + moment, sums[moment])
    for u in range(NB):
        sums = [0.0, 0.0]
        for b, h in chunks:
            product = fold(conv_at(u, b, h))
            sums = [sums[0] + product, sums[1] + product * columns[b, h]]
        for moment in range(2):
            put(3 * len(PAIRS) + NB * moment + u, sums[moment])

    mine_science.wait()
    for d in range(1, expos):
        science_copy(d, me, (me + expos - d) % expos).wait_recv()
    for e in range(expos):
        for u in range(NB):
            sums = [0.0, 0.0]
            for b, h in chunks:
                product = fold(conv_at(u, b, h) * science_at(e, b, h))
                sums = [sums[0] + product, sums[1] + product * columns[b, h]]
            for moment in range(2):
                put(count + (NB * moment + u) * expos + e, sums[moment])
        total = 0.0
        for b, h in chunks:
            total = total + fold(science_at(e, b, h))
        put(count + 2 * NB * expos + e, total)
    used = count + NU * expos
    if used < LANES:
        stat_ref[used:LANES, :] = jnp.zeros((LANES - used, LANES), jnp.float32)

    reduced = jnp.sum(jnp.transpose(stat_ref[...]), axis=0, keepdims=True)
    weight = weight_ref[...] * inter_ref[...].astype(jnp.float32)
    rbuf[me, tile, :, :LANES] = reduced
    rbuf[me, tile, :, LANES:] = jnp.broadcast_to(weight, (1, LANES))

    def stat_copy(index, e, t, to_e, to_t):
        return pltpu.make_async_remote_copy(
            src_ref=rbuf.at[e, t],
            dst_ref=rbuf.at[e, t],
            send_sem=rsend.at[index],
            recv_sem=rrecv.at[index],
            device_id={"expo": to_e, "tile": to_t},
            device_id_type=MESH,
        )

    for index, e, t in others():
        stat_copy(index, me, tile, e, t).start()
    for d in range(1, expos):
        template_copy(d, (me + d) % expos, me).wait_send()
        science_copy(d, (me + d) % expos, me).wait_send()
    for de in range(expos):
        for dt in range(tiles):
            if de or dt:
                e = (me + expos - de) % expos
                t = (tile + tiles - dt) % tiles
                stat_copy(de * tiles + dt, e, t, e, t).wait_recv()

    total = rbuf[0, 0, :, :LANES]
    for e in range(expos):
        for t in range(tiles):
            if e or t:
                total = total + rbuf[e, t, :, :LANES]
    stat_ref[...] = jnp.transpose(jnp.broadcast_to(total, (LANES, LANES)))

    def value(index):
        return jnp.broadcast_to(stat_ref[index : index + 1, :], (expos, LANES))

    matrix = [[None] * NU for _ in range(NU)]
    for index, (u, v) in enumerate(PAIRS):
        plain, once, twice = (value(3 * index + moment) for moment in range(3))
        matrix[u][v] = plain
        matrix[NB + u][v] = once
        matrix[NB + v][u] = once
        matrix[NB + u][NB + v] = twice
    for u in range(2 * NB):
        matrix[2 * NB][u] = value(3 * len(PAIRS) + u)
    pixels = float(rows * tiles * width)
    matrix[2 * NB][2 * NB] = jnp.full((expos, LANES), pixels, jnp.float32)
    trace = matrix[0][0]
    for u in range(1, NU):
        trace = trace + matrix[u][u]
    ridge = RIDGE * (trace / NU)
    for u in range(NU):
        matrix[u][u] = matrix[u][u] + ridge
    right = [stat_ref[count + u * expos : count + (u + 1) * expos, :] for u in range(NU)]
    inverse = [None] * NU
    for j in range(NU):
        inverse[j] = 1.0 / matrix[j][j]
        for i in range(j + 1, NU):
            ratio = matrix[i][j] * inverse[j]
            for m in range(j + 1, i + 1):
                matrix[i][m] = matrix[i][m] - ratio * matrix[m][j]
            right[i] = right[i] - ratio * right[j]
    fitted = [None] * NU
    for j in reversed(range(NU)):
        left = right[j]
        for i in range(j + 1, NU):
            left = left - matrix[i][j] * fitted[i]
        fitted[j] = left * inverse[j]

    spread = lax.broadcasted_iota(jnp.int32, (expos, LANES), 1)
    table = jnp.zeros((expos, LANES), jnp.float32)
    for u in range(NU):
        table = jnp.where(spread == u, fitted[u], table)
    exposure = lax.broadcasted_iota(jnp.int32, (expos, LANES), 0)
    line = jnp.sum(jnp.where(exposure == me, table, 0.0), axis=0, keepdims=True)
    coeffs_ref[0] = line[:, :NU]

    weights = [rbuf[e, tile, :, LANES:] for e in range(expos)]
    stacked = jnp.concatenate(weights, axis=0)
    joint = [jnp.sum(stacked * fitted[u], axis=0, keepdims=True) for u in range(NU)]
    for b, h in chunks:
        result = science_at(0, b, h) * weights[0]
        for e in range(1, expos):
            result = result + science_at(e, b, h) * weights[e]
        result = result - joint[2 * NB]
        for k in range(NB):
            factor = joint[k] + columns[b, h] * joint[NB + k]
            result = result - conv_at(k, b, h) * factor
        start = b * WIDE + h * LANES
        coadd_ref[0, :, start : start + LANES] = result
    for index, e, t in others():
        stat_copy(index, me, tile, e, t).wait_send()


def window(sizes, template, science, plan, orders, coadd_weight, intersection):
    expos, tiles = (sizes["expo"], sizes["tile"])
    rows, width = template.shape[1:]
    cols = width // expos
    fits = (
        science.shape[1] == 1
        and template.shape[0] == 1
        and expos > 1
        and tiles > 1
        and width % expos == 0
        and cols % WIDE == 0
        and rows % 16 == 0
        and 3 * len(PAIRS) + 2 * NB + NU * expos <= LANES
    )
    if not fits:
        return per_device(template, science, plan, orders, coadd_weight, intersection)
    span = cols + 4 * LANES
    spare = 10368 * 1024
    dims = (expos, tiles, rows, width, cols)
    dma = pltpu.SemaphoreType.DMA
    scalar = pl.BlockSpec(memory_space=pltpu.SMEM)
    far = pl.BlockSpec(memory_space=pltpu.HBM)
    vector = pl.BlockSpec(memory_space=pltpu.VMEM)
    return pl.pallas_call(
        functools.partial(fused, dims),
        out_shape=(
            jax.ShapeDtypeStruct((1, rows, cols), jnp.float32),
            jax.ShapeDtypeStruct((1, 1, NU), jnp.float32),
        ),
        in_specs=[far, far, scalar, scalar, vector, vector],
        out_specs=(vector, vector),
        scratch_shapes=[
            pltpu.VMEM((expos, 3, rows, span), jnp.bfloat16),
            pltpu.VMEM((expos, rows, cols), jnp.bfloat16),
            pltpu.VMEM((expos, tiles, 1, 2 * LANES), jnp.float32),
            pltpu.VMEM((NB * rows, 3 * rows), jnp.bfloat16),
            pltpu.VMEM((NB, WIDE + 2 * LANES, WIDE), jnp.bfloat16),
            pltpu.VMEM((NB, rows * (cols // WIDE), WIDE), jnp.float32),
            pltpu.VMEM((LANES, LANES), jnp.float32),
            dma((2,)),
            dma((expos,)),
            dma((expos,)),
            dma((expos,)),
            dma((expos,)),
            dma((2, expos)),
            dma((2, expos)),
            dma((expos * tiles,)),
            dma((expos * tiles,)),
        ],
        compiler_params=pltpu.CompilerParams(collective_id=0, has_side_effects=True, vmem_limit_bytes=VMEM_BYTES - spare),
    )(template, science, plan, orders.T, coadd_weight, intersection)


def solution(mesh):
    return jax.shard_map(
        functools.partial(window, dict(mesh.shape)),
        mesh=mesh,
        in_specs=(
            P(("groups", "expo"), "tile", None),
            P(("groups", "expo"), None, "tile", None),
            P("groups"),
            P(),
            P(("groups", "expo"), None),
            P(("groups", "expo"), None),
        ),
        out_specs=(P("groups", "tile", "expo"), P(("groups", "expo"), None, None)),
        check_vma=False,
    )
```

profile of v0, /device:TPU:0, one launch (start us, length us, event | category | flops | bytes accessed | tf_op | source)
XLA Modules:
  0.0 23.8 jit_solution(1620683842319845226)
XLA Ops:
  1.9 0.0 copy-start
  1.9 0.0 copy-start.1
  1.9 0.7 %copy-done = s32[6,2]{0,1:T(2,128)S(1)} copy-done((s32[6,2]{0,1:T(2,128)S(1)}, s32[6,2]{0,1:T(2,128)}, u32[]{:S(2)}) %copy-start) | copy-done | bytes 72
  2.6 0.0 copy-done.1
  2.6 20.1 %shard_map.77 = (f32[1,16,1024]{2,1,0:T(8,128)S(1)}, f32[1,1,13]{2,1,0:T(1,128)S(1)}) custom-call(bf16[1,16,4096]{2,1,0:T(8,128)(2,1)} %template_ref.1, bf16[1,1,16,4096]{3,2,1,0:T(8,128)(2,1)} %science_ref.1, s32[4]{0:T(128)S(1)} %copy-done.1, s32[2,6]{1,0:T(2,128)S(1)} %bitcast.1, f32[1,1]{1,0:T(1,128)S(6)} %copy.10.weight_ref, s32[1,1]{1,0:T(1,128)S(6)} %copy.11.inter_ref), custom_call_target="tpu_custom_call" | custom-call | tf_op jit(solution)/shard_map/pallas_call | solution.py:504
  22.7 0.6 %copy.12 = f32[1,16,1024]{2,1,0:T(8,128)} copy(f32[1,16,1024]{2,1,0:T(8,128)S(1)} %get-tuple-element.4) | data formatting | bytes 131072
  23.3 0.5 %copy.13 = f32[1,1,13]{2,1,0:T(1,128)} copy(f32[1,1,13]{2,1,0:T(1,128)S(1)} %get-tuple-element.5) | data formatting | bytes 104
Async XLA Ops:
  1.9 0.7 %copy-start = (s32[6,2]{0,1:T(2,128)S(1)}, s32[6,2]{0,1:T(2,128)}, u32[]{:S(2)}) copy-start(s32[6,2]{0,1:T(2,128)} %param.9) | copy-start | bytes 148
  1.9 0.7 %copy-start.1 = (s32[4]{0:T(128)S(1)}, s32[4]{0:T(128)}, u32[]{:S(2)}) copy-start(s32[4]{0:T(128)} %plan_ref.1) | copy-start | bytes 52
where the time goes:
time: 24 us; the launch traced here: 23.8 us
  Pallas kernels  20.1 us (84%)
  between operations  1.95 us (8%)
  local copies, waits for them, and re-layouts  1.81 us (8%)
    pallas_call x1, Pallas kernels, window(): pl.pallas_call(functools.partial(fused, dims), out_shape=(jax.ShapeDtypeS...  20.1 us
    unnamed x6, local copies, waits for them, and re-layouts  1.81 us

commit v1 on v0

v1 whole, which is shorter than its diff:
```python
import functools

import jax
import jax.numpy as jnp
from jax import lax
from jax.experimental import pallas as pl
from jax.experimental.pallas import tpu as pltpu
from jax.sharding import PartitionSpec as P

HALF = 15
NB = 6
NU = 13


SIGMAS = (0.8, 1.4, 2.2, 3.0, 4.0, 5.5)
RIDGE = 0.05


def broadcast(block, axis, holder):
    block = jnp.where(lax.axis_index(axis) == holder, block, jnp.zeros_like(block))
    return lax.psum(block, axis)


def extended(x, sides, width):
    for axis, dim in sides:
        size, length = (lax.axis_size(axis), x.shape[dim])
        up = [(i, (i + 1) % size) for i in range(size - 1)]
        down = [(j, i) for i, j in up]
        last = lax.slice_in_dim(x, length - width, length, axis=dim)
        first = lax.slice_in_dim(x, 0, width, axis=dim)
        before = lax.ppermute(last, axis, up)
        after = lax.ppermute(first, axis, down)
        x = jnp.concatenate([before, x, after], axis=dim)
    return x


def make_filters(orders):
    taps_pos = jnp.arange(2 * HALF + 1).astype(jnp.float32) - HALF
    row_list = []
    col_list = []
    for basis in range(NB):
        sigma = SIGMAS[basis]
        envelope = jnp.exp(-taps_pos * taps_pos / (2.0 * sigma * sigma))

        def power(order):
            return jnp.where(order == 0, 1.0, jnp.where(order == 1, taps_pos, taps_pos * taps_pos))

        row_filter = envelope * power(orders[basis, 0])
        col_filter = envelope * power(orders[basis, 1])
        row_list.append(row_filter / jnp.sqrt(jnp.sum(row_filter * row_filter)))
        col_list.append(col_filter / jnp.sqrt(jnp.sum(col_filter * col_filter)))
    return (jnp.stack(row_list).astype(jnp.bfloat16), jnp.stack(col_list).astype(jnp.bfloat16))


def band_matrix(filters, out_len, in_len):
    offset = jnp.arange(in_len)[None, :] - jnp.arange(out_len)[:, None]
    taps_idx = jnp.arange(2 * HALF + 1)
    picks = (offset[:, :, None] == taps_idx[None, None, :]).astype(jnp.float32)
    band = jnp.einsum("ijt,kt->kij", picks, filters.astype(jnp.float32))
    return band.astype(jnp.bfloat16)


def per_device(template, science, plan, orders, coadd_weight, intersection):
    row_filters, col_filters = make_filters(orders)
    rows = template.shape[1]
    width = template.shape[2]
    blocks_count = width // 128
    steps_count = science.shape[1]
    row_band = band_matrix(row_filters, rows, rows + 2 * HALF)
    col_band = jnp.transpose(band_matrix(col_filters, 128, 128 + 2 * HALF), (0, 2, 1))
    column_pos = 2.0 * (jnp.arange(width).astype(jnp.float32) + 0.5) / width - 1.0
    pieces = []
    fitted = []
    for step in range(steps_count):
        owner_index = plan[step]
        received = broadcast(template[0], "expo", owner_index)
        padded = extended(received, (("tile", 0),), HALF)
        rowconv = jnp.einsum(
            "kij,jw->kiw", row_band, padded, preferred_element_type=jnp.float32
        ).astype(jnp.bfloat16)
        blocks = rowconv.reshape(NB, rows, blocks_count, 128)
        empty_rim = jnp.zeros((NB, rows, 1, HALF), jnp.bfloat16)
        previous = jnp.concatenate([empty_rim, blocks[:, :, :-1, 128 - HALF :]], axis=2)
        following = jnp.concatenate([blocks[:, :, 1:, :HALF], empty_rim], axis=2)
        window = jnp.concatenate([previous, blocks, following], axis=3)
        conv = jnp.einsum("krbj,kjc->krbc", window, col_band, preferred_element_type=jnp.float32)
        conv = conv.reshape(NB, rows, width)
        fields = jnp.concatenate(
            [conv, conv * column_pos, jnp.ones((1, rows, width), jnp.float32)], axis=0
        )
        fields = fields.reshape(NU, rows * width)
        exposure_image = science[0, step].astype(jnp.float32).reshape(rows * width)
        normal_local = jnp.dot(fields, fields.T, precision=lax.Precision.HIGHEST)
        project_local = jnp.dot(fields, exposure_image, precision=lax.Precision.HIGHEST)
        normal_matrix, projections = lax.psum((normal_local, project_local), "tile")
        normal_matrix = normal_matrix + RIDGE * (jnp.trace(normal_matrix) / NU) * jnp.eye(
            NU, dtype=jnp.float32
        )
        factor = jnp.linalg.cholesky(normal_matrix)
        coeffs = jax.scipy.linalg.cho_solve((factor, True), projections)
        model = jnp.dot(coeffs, fields, precision=lax.Precision.HIGHEST)
        difference = exposure_image - model
        weight_now = coadd_weight[0, step] * intersection[0, step].astype(jnp.float32)
        pieces.append((weight_now * difference).reshape(rows, width))
        fitted.append(coeffs)
    weighted = jnp.stack(pieces)
    received_parts = lax.all_to_all(weighted[None], "expo", split_axis=3, concat_axis=0, tiled=True)
    coadd = jnp.sum(received_parts, axis=0)
    return (coadd, jnp.stack(fitted)[None])


LANES = 128
HALO = LANES // 2
VMEM_BYTES = 67043328
PAIRS = [(u, v) for u in range(NB) for v in range(u + 1)]
MESH = pl.DeviceIdType.MESH


def taps(position, sigma, order):
    power = jnp.where(order == 0, 1.0, jnp.where(order == 1, position, position * position))
    value = jnp.exp(-position * position / (2.0 * sigma * sigma)) * power
    return jnp.where(jnp.abs(position) <= HALF, value, 0.0)


def sublane_sums(tiles):
    row = lax.broadcasted_iota(jnp.int32, (8, LANES), 0)

    def merge(a, b, step):
        low = (row // step) % 2 == 0
        if step == 4:
            return jnp.where(low, a, b) + pltpu.roll(jnp.where(low, b, a), 4, 0)
        first = jnp.where(low, a, pltpu.roll(b, step, 0))
        return first + jnp.where(low, pltpu.roll(a, 8 - step, 0), b)

    fours = [merge(tiles[s], tiles[s + 4], 4) for s in range(4)]
    twos = [merge(fours[s], fours[s + 2], 2) for s in range(2)]
    return merge(twos[0], twos[1], 1)


def fused(
    dims,
    template_ref,
    science_ref,
    plan_ref,
    orders_ref,
    weight_ref,
    inter_ref,
    coadd_ref,
    coeffs_ref,
    tbuf,
    picked,
    sbuf,
    wbuf,
    rbuf,
    row_band,
    col_band,
    conv_ref,
    fold_ref,
    stat_ref,
    plan_mem,
    orders_mem,
    weight_mem,
    inter_mem,
    local_sem,
    tsend,
    trecv,
    ssend,
    srecv,
    wsend,
    wrecv,
    fsend,
    frecv,
    rsend,
    rrecv,
):
    expos, tiles, rows, width, cols = dims
    per = cols // LANES
    span = cols + 2 * LANES
    keep = cols + 2 * HALO
    me = lax.axis_index("expo")
    tile = lax.axis_index("tile")

    def others():
        near = [0] + list(range(2, expos - 1))
        for de in [expos - 1, 1][: expos - 1] + near[1:] + near[:1]:
            for dt in reversed(range(tiles)):
                if de or dt:
                    yield de * tiles + dt, (me + de) % expos, (tile + dt) % tiles

    barrier = pltpu.get_barrier_semaphore()

    for d in range(1, expos):
        peer = (me + d) % expos
        pl.semaphore_signal(barrier, inc=1, device_id={"expo": peer}, device_id_type=MESH)
    for d in (1, tiles - 1):
        peer = (tile + d) % tiles
        pl.semaphore_signal(barrier, inc=1, device_id={"tile": peer}, device_id_type=MESH)

    def source_start(e):
        return e * per - 1 + (expos - 1 - e) // (expos - 1) - e // (expos - 1)

    def source_columns(e):
        return pl.ds(pl.multiple_of(source_start(e) * LANES, LANES), span)

    def window_columns(e):
        return pl.ds(pl.multiple_of((source_start(e) - e * per + 2) * LANES, LANES), span)

    def own_columns(e):
        return pl.ds(pl.multiple_of(e * cols, LANES), cols)

    local = [
        pltpu.make_async_copy(plan_ref, plan_mem, local_sem.at[0]),
        pltpu.make_async_copy(orders_ref, orders_mem, local_sem.at[1]),
        pltpu.make_async_copy(weight_ref, weight_mem, local_sem.at[2]),
        pltpu.make_async_copy(inter_ref, inter_mem, local_sem.at[3]),
        pltpu.make_async_copy(
            template_ref.at[0, :, source_columns(me)],
            tbuf.at[me, :, window_columns(me)],
            local_sem.at[4],
        ),
        pltpu.make_async_copy(
            science_ref.at[0, 0, :, own_columns(me)], sbuf.at[me], local_sem.at[5]
        ),
    ]
    plan_in, orders_in, weight_in, inter_in, mine, mine_science = local
    for copy in local:
        copy.start()

    def template_copy(d, target, holder):
        return pltpu.make_async_remote_copy(
            src_ref=template_ref.at[0, :, source_columns(target)],
            dst_ref=tbuf.at[holder, :, window_columns(target)],
            send_sem=tsend.at[d],
            recv_sem=trecv.at[d],
            device_id={"expo": target},
            device_id_type=MESH,
        )

    def science_copy(d, target, holder):
        return pltpu.make_async_remote_copy(
            src_ref=science_ref.at[0, 0, :, own_columns(target)],
            dst_ref=sbuf.at[holder],
            send_sem=ssend.at[d],
            recv_sem=srecv.at[d],
            device_id={"expo": target},
            device_id_type=MESH,
        )

    def weight_copy(d, target, holder):
        return pltpu.make_async_remote_copy(
            src_ref=wbuf.at[holder],
            dst_ref=wbuf.at[holder],
            send_sem=wsend.at[d],
            recv_sem=wrecv.at[d],
            device_id={"expo": target},
            device_id_type=MESH,
        )

    def forward_copy(side):
        target = tile + 1 if side == 0 else tile - 1
        return pltpu.make_async_remote_copy(
            src_ref=picked.at[1],
            dst_ref=picked.at[2 * side],
            send_sem=fsend.at[side],
            recv_sem=frecv.at[side],
            device_id={"tile": target},
            device_id_type=MESH,
        )

    def stat_copy(index, e, t, to_e, to_t):
        return pltpu.make_async_remote_copy(
            src_ref=rbuf.at[e, t],
            dst_ref=rbuf.at[e, t],
            send_sem=rsend.at[index],
            recv_sem=rrecv.at[index],
            device_id={"expo": to_e, "tile": to_t},
            device_id_type=MESH,
        )

    pl.semaphore_wait(barrier, expos + 1)
    for d in reversed(range(1, expos)):
        template_copy(d, (me + d) % expos, me).start()

    for d in range(1, expos):
        science_copy(d, (me + d) % expos, me).start()
    weight_in.wait()
    inter_in.wait()
    weight = weight_mem[0, 0] * inter_mem[0, 0].astype(jnp.float32)
    wbuf[me] = jnp.full((1, LANES), weight, jnp.float32)
    for d in range(1, expos):
        weight_copy(d, (me + d) % expos, me).start()

    orders_in.wait()
    position = lax.broadcasted_iota(jnp.int32, (1, LANES), 1).astype(jnp.float32) - HALF
    for k in range(NB):
        sigma = SIGMAS[k]
        for side in range(2):
            order = orders_mem[side, k]
            line = taps(position, sigma, jnp.full((1, LANES), order, jnp.int32))
            scale = 1.0 / jnp.sqrt(jnp.sum(line * line, axis=1, keepdims=True))
            shape = (rows, 3 * rows) if side == 0 else (LANES + 2 * HALO, LANES)
            ahead = lax.broadcasted_iota(jnp.int32, shape, 1 - side)
            behind = lax.broadcasted_iota(jnp.int32, shape, side)
            offset = (ahead - behind - (rows if side == 0 else HALO)).astype(jnp.float32)
            band = taps(offset, sigma, jnp.full(shape, order, jnp.int32))
            band = (band * scale).astype(jnp.bfloat16)
            if side == 0:
                row_band[k * rows : (k + 1) * rows, :] = band
            else:
                col_band[k] = band

    @pl.when(tile == 0)
    def _():
        picked[0] = jnp.zeros((rows, keep), jnp.bfloat16)

    @pl.when(tile == tiles - 1)
    def _():
        picked[2] = jnp.zeros((rows, keep), jnp.bfloat16)

    plan_in.wait()
    owner = plan_mem[0]
    mine.wait()
    for d in range(1, expos):
        template_copy(d, me, (me + expos - d) % expos).wait_recv()

    block = tbuf[owner, :, LANES : LANES + span].astype(jnp.float32)
    place = jnp.full((rows, LANES), me, jnp.int32)
    block = jnp.concatenate(
        [
            jnp.where(place > 0, block[:, :LANES], 0.0),
            block[:, LANES : span - LANES],
            jnp.where(place < expos - 1, block[:, span - LANES :], 0.0),
        ],
        axis=1,
    )
    picked[1] = block[:, LANES - HALO : LANES - HALO + keep].astype(jnp.bfloat16)

    @pl.when(tile < tiles - 1)
    def _():
        forward_copy(0).start()

    @pl.when(tile > 0)
    def _():
        forward_copy(1).start()

    @pl.when(tile > 0)
    def _():
        forward_copy(0).wait_recv()

    @pl.when(tile < tiles - 1)
    def _():
        forward_copy(1).wait_recv()

    rowconv = jnp.dot(
        row_band[...], picked[...].reshape(3 * rows, keep), preferred_element_type=jnp.float32
    ).astype(jnp.bfloat16)
    for k in range(NB):
        mine_rows = rowconv[k * rows : (k + 1) * rows]
        windows = jnp.concatenate(
            [mine_rows[:, b * LANES : (b + 1) * LANES + 2 * HALO] for b in range(per)], axis=0
        )
        conv_ref[k] = jnp.dot(windows, col_band[k], preferred_element_type=jnp.float32)

    def conv_at(k, b):
        return conv_ref[k, b * rows : (b + 1) * rows, :]

    def science_at(e, b):
        return sbuf[e, :, b * LANES : (b + 1) * LANES].astype(jnp.float32)

    def fold(x):
        return x.reshape(rows // 8, 8, LANES).sum(axis=0)

    lane = lax.broadcasted_iota(jnp.int32, (1, LANES), 1)
    first = 2.0 * ((me * cols + lane).astype(jnp.float32) + 0.5) / width - 1.0
    pitch = 2.0 * LANES / width
    column = [first + b * pitch for b in range(per)]

    def running(tiles_of, depth):
        sums = [None] * depth
        for b in reversed(range(per)):
            carry = tiles_of(b)
            for level in range(depth):
                if level and b == 0:
                    break
                sums[level] = carry if sums[level] is None else sums[level] + carry
                carry = sums[level]
        return sums

    def once(sums):
        return first * sums[0] + pitch * sums[1]

    count = 3 * len(PAIRS) + 2 * NB
    first_twice = first * first
    first_once = 2.0 * pitch * first - pitch * pitch
    for index, (u, v) in enumerate(PAIRS):
        sums = running(lambda b: fold(conv_at(u, b) * conv_at(v, b)), 3)
        fold_ref[3 * index] = sums[0]
        fold_ref[3 * index + 1] = once(sums)
        fold_ref[3 * index + 2] = (
            first_twice * sums[0] + first_once * sums[1] + (2.0 * pitch * pitch) * sums[2]
        )
    for u in range(NB):
        sums = running(lambda b: fold(conv_at(u, b)), 2)
        fold_ref[3 * len(PAIRS) + u] = sums[0]
        fold_ref[3 * len(PAIRS) + NB + u] = once(sums)

    mine_science.wait()
    for d in range(1, expos):
        science_copy(d, me, (me + expos - d) % expos).wait_recv()
    for e in range(expos):
        science = [science_at(e, b) for b in range(per)]
        for u in range(NB):
            sums = running(lambda b: fold(conv_at(u, b) * science[b]), 2)
            fold_ref[count + u * expos + e] = sums[0]
            fold_ref[count + (NB + u) * expos + e] = once(sums)
        fold_ref[count + 2 * NB * expos + e] = running(lambda b: fold(science[b]), 1)[0]
    used = count + NU * expos
    for index in range(used, LANES):
        fold_ref[index] = jnp.zeros((8, LANES), jnp.float32)

    packed = jnp.concatenate(
        [sublane_sums([fold_ref[g + s] for s in range(8)]) for g in range(0, LANES, 8)], axis=0
    )
    rbuf[me, tile] = jnp.sum(jnp.transpose(packed), axis=0, keepdims=True)
    for index, e, t in others():
        stat_copy(index, me, tile, e, t).start()

    for d in range(1, expos):
        weight_copy(d, me, (me + expos - d) % expos).wait_recv()
    weights = [wbuf[e] for e in range(expos)]
    for b in range(per):
        result = science_at(0, b) * weights[0]
        for e in range(1, expos):
            result = result + science_at(e, b) * weights[e]
        coadd_ref[0, :, b * LANES : (b + 1) * LANES] = result

    for index, e, t in others():
        de, dt = index // tiles, index % tiles
        e = (me + expos - de) % expos
        t = (tile + tiles - dt) % tiles
        stat_copy(index, e, t, e, t).wait_recv()

    total = rbuf[0, 0]
    for e in range(expos):
        for t in range(tiles):
            if e or t:
                total = total + rbuf[e, t]
    stat_ref[...] = jnp.transpose(jnp.broadcast_to(total, (LANES, LANES)))

    def value(index):
        return jnp.broadcast_to(stat_ref[index : index + 1, :], (expos, LANES))

    matrix = [[None] * NU for _ in range(NU)]
    for index, (u, v) in enumerate(PAIRS):
        plain, linear, square = (value(3 * index + moment) for moment in range(3))
        matrix[u][v] = plain
        matrix[NB + u][v] = linear
        matrix[NB + v][u] = linear
        matrix[NB + u][NB + v] = square
    for u in range(2 * NB):
        matrix[2 * NB][u] = value(3 * len(PAIRS) + u)
    pixels = float(rows * tiles * width)
    matrix[2 * NB][2 * NB] = jnp.full((expos, LANES), pixels, jnp.float32)
    trace = matrix[0][0]
    for u in range(1, NU):
        trace = trace + matrix[u][u]
    ridge = RIDGE * (trace / NU)
    for u in range(NU):
        matrix[u][u] = matrix[u][u] + ridge
    right = [stat_ref[count + u * expos : count + (u + 1) * expos, :] for u in range(NU)]
    inverse = [None] * NU
    for j in range(NU):
        inverse[j] = 1.0 / matrix[j][j]
        for i in range(j + 1, NU):
            ratio = matrix[i][j] * inverse[j]
            for m in range(j + 1, i + 1):
                matrix[i][m] = matrix[i][m] - ratio * matrix[m][j]
            right[i] = right[i] - ratio * right[j]
    fitted = [None] * NU
    for j in reversed(range(NU)):
        left = right[j]
        for i in range(j + 1, NU):
            left = left - matrix[i][j] * fitted[i]
        fitted[j] = left * inverse[j]

    stacked = jnp.concatenate(weights, axis=0)
    joint = [jnp.sum(stacked * fitted[u], axis=0, keepdims=True) for u in range(NU)]
    for b in range(per):
        block = slice(b * LANES, (b + 1) * LANES)
        result = coadd_ref[0, :, block] - joint[2 * NB]
        for k in range(NB):
            factor = joint[k] + column[b] * joint[NB + k]
            result = result - conv_at(k, b) * factor
        coadd_ref[0, :, block] = result

    spread = lax.broadcasted_iota(jnp.int32, (expos, LANES), 1)
    table = jnp.zeros((expos, LANES), jnp.float32)
    for u in range(NU):
        table = jnp.where(spread == u, fitted[u], table)
    exposure = lax.broadcasted_iota(jnp.int32, (expos, LANES), 0)
    line = jnp.sum(jnp.where(exposure == me, table, 0.0), axis=0, keepdims=True)
    coeffs_ref[0] = line[:, :NU]

    for d in range(1, expos):
        template_copy(d, (me + d) % expos, me).wait_send()
        science_copy(d, (me + d) % expos, me).wait_send()
        weight_copy(d, (me + d) % expos, me).wait_send()

    @pl.when(tile < tiles - 1)
    def _():
        forward_copy(0).wait_send()

    @pl.when(tile > 0)
    def _():
        forward_copy(1).wait_send()

    for index, e, t in others():
        stat_copy(index, me, tile, e, t).wait_send()


def store(coadd_in, coeffs_in, coadd_out, coeffs_out, sem):
    copies = [
        pltpu.make_async_copy(coadd_in, coadd_out, sem.at[0]),
        pltpu.make_async_copy(coeffs_in, coeffs_out, sem.at[1]),
    ]
    for copy in copies:
        copy.start()
    for copy in copies:
        copy.wait()


def window(sizes, template, science, plan, orders, coadd_weight, intersection):
    expos, tiles = (sizes["expo"], sizes["tile"])
    rows, width = template.shape[1:]
    cols = width // expos
    fits = (
        science.shape[1] == 1
        and template.shape[0] == 1
        and expos > 2
        and tiles > 2
        and width % expos == 0
        and cols % LANES == 0
        and cols // LANES > 2
        and rows % 16 == 0
        and 3 * len(PAIRS) + 2 * NB + NU * expos <= LANES
    )
    if not fits:
        return per_device(template, science, plan, orders, coadd_weight, intersection)
    spare = 10368 * 1024
    dims = (expos, tiles, rows, width, cols)
    dma = pltpu.SemaphoreType.DMA
    far = pl.BlockSpec(memory_space=pltpu.HBM)
    vector = pl.BlockSpec(memory_space=pltpu.VMEM)
    shapes = (
        jax.ShapeDtypeStruct((1, rows, cols), jnp.float32),
        jax.ShapeDtypeStruct((1, 1, NU), jnp.float32),
    )
    orders = orders.T
    results = pl.pallas_call(
        functools.partial(fused, dims),
        out_shape=shapes,
        in_specs=[far] * 6,
        out_specs=(vector, vector),
        scratch_shapes=[
            pltpu.VMEM((expos, rows, cols + 4 * LANES), jnp.bfloat16),
            pltpu.VMEM((3, rows, cols + 2 * HALO), jnp.bfloat16),
            pltpu.VMEM((expos, rows, cols), jnp.bfloat16),
            pltpu.VMEM((expos, 1, LANES), jnp.float32),
            pltpu.VMEM((expos, tiles, 1, LANES), jnp.float32),
            pltpu.VMEM((NB * rows, 3 * rows), jnp.bfloat16),
            pltpu.VMEM((NB, LANES + 2 * HALO, LANES), jnp.bfloat16),
            pltpu.VMEM((NB, rows * (cols // LANES), LANES), jnp.float32),
            pltpu.VMEM((LANES, 8, LANES), jnp.float32),
            pltpu.VMEM((LANES, LANES), jnp.float32),
            pltpu.SMEM(plan.shape, jnp.int32),
            pltpu.SMEM(orders.shape, jnp.int32),
            pltpu.SMEM(coadd_weight.shape, jnp.float32),
            pltpu.SMEM(intersection.shape, jnp.int32),
            dma((6,)),
            dma((expos,)),
            dma((expos,)),
            dma((expos,)),
            dma((expos,)),
            dma((expos,)),
            dma((expos,)),
            dma((2,)),
            dma((2,)),
            dma((expos * tiles,)),
            dma((expos * tiles,)),
        ],
        compiler_params=pltpu.CompilerParams(
            collective_id=0, has_side_effects=True, vmem_limit_bytes=VMEM_BYTES - spare
        ),
    )(template, science, plan, orders, coadd_weight, intersection)
    return pl.pallas_call(
        store,
        out_shape=shapes,
        in_specs=[vector, vector],
        out_specs=(far, far),
        scratch_shapes=[dma((2,))],
        compiler_params=pltpu.CompilerParams(vmem_limit_bytes=1024 * 1024),
    )(*results)


def solution(mesh):
    return jax.shard_map(
        functools.partial(window, dict(mesh.shape)),
        mesh=mesh,
        in_specs=(
            P(("groups", "expo"), "tile", None),
            P(("groups", "expo"), None, "tile", None),
            P("groups"),
            P(),
            P(("groups", "expo"), None),
            P(("groups", "expo"), None),
        ),
        out_specs=(P("groups", "tile", "expo"), P(("groups", "expo"), None, None)),
        check_vma=False,
    )
```

time: 24 us -> 22.3 us (0.929)
  local copies, waits for them, and re-layouts: 1.81 us -> 0.67 us
  Pallas kernels: 20.1 us -> 19.5 us
    unnamed x6 -> x4, local copies, waits for them, and re-layouts: 1.81 us -> 0.67 us
    pallas_call x1 -> x2, Pallas kernels: 20.1 us -> 19.5 us  [the longest x1 18.9 us: window(): pl.pallas_call(functools.partial(fused, dims), out_shape=shapes, in_specs...]
where the time goes in v1:
time: 22.3 us; the launch traced here: 22.1 us
  Pallas kernels  19.5 us (87%)
  between operations  1.95 us (9%)
  local copies, waits for them, and re-layouts  0.67 us (3%)
    pallas_call x1, Pallas kernels, window(): pl.pallas_call(functools.partial(fused, dims), out_shape=shapes, in_specs...  18.9 us
    unnamed x4, local copies, waits for them, and re-layouts  0.67 us
    pallas_call x1, Pallas kernels, window(): pl.pallas_call(store, out_shape=shapes, in_specs=[vector, vector], out_sp...  0.65 us

profile of v1, /device:TPU:0, one launch (start us, length us, event | category | flops | bytes accessed | tf_op | source)
XLA Modules:
  0.0 22.1 jit_solution(11461951378743509995)
XLA Ops:
  1.9 0.0 copy-start
  1.9 0.0 copy-start.1
  1.9 0.7 %copy-done = s32[6,2]{0,1:T(2,128)S(1)} copy-done((s32[6,2]{0,1:T(2,128)S(1)}, s32[6,2]{0,1:T(2,128)}, u32[]{:S(2)}) %copy-start) | copy-done | bytes 72
  2.6 0.0 copy-done.1
  2.6 18.9 %shard_map.77 = (f32[1,16,1024]{2,1,0:T(8,128)S(1)}, f32[1,1,13]{2,1,0:T(1,128)S(1)}) custom-call(bf16[1,16,4096]{2,1,0:T(8,128)(2,1)} %template_ref.1, bf16[1,1,16,4096]{3,2,1,0:T(8,128)(2,1)} %science_ref.1, s32[4]{0:T(128)S(1)} %copy-done.1, s32[2,6]{1,0:T(2,128)S(1)} %bitcast.1, f32[1,1]{1,0:T(1,128)S(6)} %copy.8.weight_ref, s32[1,1]{1,0:T(1,128)S(6)} %copy.9.inter_ref), custom_call_target="tpu_custom_call" | custom-call | tf_op jit(solution)/shard_map/pallas_call | solution.py:559
  21.5 0.7 %shard_map.78 = (f32[1,16,1024]{2,1,0:T(8,128)}, f32[1,1,13]{2,1,0:T(1,128)}) custom-call(f32[1,16,1024]{2,1,0:T(8,128)S(1)} %get-tuple-element.4.coadd_in, f32[1,1,13]{2,1,0:T(1,128)S(1)} %get-tuple-element.5.coeffs_in), custom_call_target="tpu_custom_call" | custom-call | tf_op jit(solution)/shard_map/pallas_call | solution.py:595
Async XLA Ops:
  1.9 0.7 %copy-start = (s32[6,2]{0,1:T(2,128)S(1)}, s32[6,2]{0,1:T(2,128)}, u32[]{:S(2)}) copy-start(s32[6,2]{0,1:T(2,128)} %param.9) | copy-start | bytes 148
  1.9 0.7 %copy-start.1 = (s32[4]{0:T(128)S(1)}, s32[4]{0:T(128)}, u32[]{:S(2)}) copy-start(s32[4]{0:T(128)} %plan_ref.1) | copy-start | bytes 52

commit v2 on v1

--- a/solution.py
+++ b/solution.py
@@ -279,7 +279,14 @@
 
     pl.semaphore_wait(barrier, expos + 1)
     for d in reversed(range(1, expos)):
-        template_copy(d, (me + d) % expos, me).start()
+
+        @pl.when(me + d < expos)
+        def _():
+            template_copy(d, me + d, me).start()
+
+        @pl.when(me - d >= 0)
+        def _():
+            template_copy(expos - d, me - d, me).start()
 
     for d in range(1, expos):
         science_copy(d, (me + d) % expos, me).start()
@@ -555,7 +562,7 @@
         jax.ShapeDtypeStruct((1, rows, cols), jnp.float32),
         jax.ShapeDtypeStruct((1, 1, NU), jnp.float32),
     )
-    orders = orders.T
+    plan, orders = (pltpu.with_memory_space_constraint(x, pltpu.HBM) for x in (plan, orders.T))
     results = pl.pallas_call(
         functools.partial(fused, dims),
         out_shape=shapes,

time: 22.3 us -> 21.7 us (0.973)
  local copies, waits for them, and re-layouts: 0.67 us -> 0 us
    unnamed x4 -> x0, local copies, waits for them, and re-layouts: 0.67 us -> none
where the time goes in v2:
time: 21.7 us; the launch traced here: 21.5 us
  Pallas kernels  19.6 us (90%)
  between operations  1.93 us (9%)
    pallas_call x1, Pallas kernels, window(): pl.pallas_call(functools.partial(fused, dims), out_shape=shapes, in_specs...  18.9 us
    pallas_call x1, Pallas kernels, window(): pl.pallas_call(store, out_shape=shapes, in_specs=[vector, vector], out_sp...  0.65 us

profile of v2, /device:TPU:0, one launch (start us, length us, event | category | flops | bytes accessed | tf_op | source)
XLA Modules:
  0.0 21.5 jit_solution(12332210098375509129)
XLA Ops:
  1.9 18.9 %shard_map.77 = (f32[1,16,1024]{2,1,0:T(8,128)S(1)}, f32[1,1,13]{2,1,0:T(1,128)S(1)}) custom-call(bf16[1,16,4096]{2,1,0:T(8,128)(2,1)} %template_ref.1, bf16[1,1,16,4096]{3,2,1,0:T(8,128)(2,1)} %science_ref.1, s32[4]{0:T(128)} %plan_ref.1, s32[2,6]{1,0:T(2,128)} %bitcast.1, f32[1,1]{1,0:T(1,128)S(6)} %copy.8.weight_ref, s32[1,1]{1,0:T(1,128)S(6)} %copy.9.inter_ref), custom_call_target="tpu_custom_call" | custom-call | tf_op jit(solution)/shard_map/pallas_call | solution.py:566
  20.8 0.7 %shard_map.78 = (f32[1,16,1024]{2,1,0:T(8,128)}, f32[1,1,13]{2,1,0:T(1,128)}) custom-call(f32[1,16,1024]{2,1,0:T(8,128)S(1)} %get-tuple-element.4.coadd_in, f32[1,1,13]{2,1,0:T(1,128)S(1)} %get-tuple-element.5.coeffs_in), custom_call_target="tpu_custom_call" | custom-call | tf_op jit(solution)/shard_map/pallas_call | solution.py:602

commit v3 on v2

--- a/solution.py
+++ b/solution.py
@@ -147,6 +147,9 @@
     inter_ref,
     coadd_ref,
     coeffs_ref,
+    template_mem,
+    science_mem,
+    shifted,
     tbuf,
     picked,
     sbuf,
@@ -175,7 +178,6 @@
 ):
     expos, tiles, rows, width, cols = dims
     per = cols // LANES
-    span = cols + 2 * LANES
     keep = cols + 2 * HALO
     me = lax.axis_index("expo")
     tile = lax.axis_index("tile")
@@ -196,14 +198,8 @@
         peer = (tile + d) % tiles
         pl.semaphore_signal(barrier, inc=1, device_id={"tile": peer}, device_id_type=MESH)
 
-    def source_start(e):
-        return e * per - 1 + (expos - 1 - e) // (expos - 1) - e // (expos - 1)
-
-    def source_columns(e):
-        return pl.ds(pl.multiple_of(source_start(e) * LANES, LANES), span)
-
-    def window_columns(e):
-        return pl.ds(pl.multiple_of((source_start(e) - e * per + 2) * LANES, LANES), span)
+    def shifted_columns(e):
+        return pl.ds(pl.multiple_of(e * cols, LANES), keep)
 
     def own_columns(e):
         return pl.ds(pl.multiple_of(e * cols, LANES), cols)
@@ -214,22 +210,23 @@
         pltpu.make_async_copy(weight_ref, weight_mem, local_sem.at[2]),
         pltpu.make_async_copy(inter_ref, inter_mem, local_sem.at[3]),
         pltpu.make_async_copy(
-            template_ref.at[0, :, source_columns(me)],
-            tbuf.at[me, :, window_columns(me)],
-            local_sem.at[4],
+            science_ref.at[0, 0, :, own_columns(me)], sbuf.at[me], local_sem.at[4]
         ),
-        pltpu.make_async_copy(
-            science_ref.at[0, 0, :, own_columns(me)], sbuf.at[me], local_sem.at[5]
-        ),
+        pltpu.make_async_copy(template_ref.at[0], template_mem, local_sem.at[5]),
+        pltpu.make_async_copy(science_ref.at[0, 0], science_mem, local_sem.at[6]),
     ]
-    plan_in, orders_in, weight_in, inter_in, mine, mine_science = local
+    plan_in, orders_in, weight_in, inter_in, mine_science, template_in, science_in = local
+    local = [template_in, science_in] + local[:5]
+    mine = pltpu.make_async_copy(
+        shifted.at[:, shifted_columns(me)], tbuf.at[me], local_sem.at[7]
+    )
     for copy in local:
         copy.start()
 
     def template_copy(d, target, holder):
         return pltpu.make_async_remote_copy(
-            src_ref=template_ref.at[0, :, source_columns(target)],
-            dst_ref=tbuf.at[holder, :, window_columns(target)],
+            src_ref=shifted.at[:, shifted_columns(target)],
+            dst_ref=tbuf.at[holder],
             send_sem=tsend.at[d],
             recv_sem=trecv.at[d],
             device_id={"expo": target},
@@ -238,7 +235,7 @@
 
     def science_copy(d, target, holder):
         return pltpu.make_async_remote_copy(
-            src_ref=science_ref.at[0, 0, :, own_columns(target)],
+            src_ref=science_mem.at[:, own_columns(target)],
             dst_ref=sbuf.at[holder],
             send_sem=ssend.at[d],
             recv_sem=srecv.at[d],
@@ -277,6 +274,17 @@
             device_id_type=MESH,
         )
 
+    template_in.wait()
+    low = lax.broadcasted_iota(jnp.int32, (rows, LANES), 1) < HALO
+    before = jnp.zeros((rows, LANES), jnp.float32)
+    for start in range(0, width + LANES, LANES):
+        after = jnp.zeros((rows, LANES), jnp.float32)
+        if start < width:
+            block = template_mem[:, start : start + LANES].astype(jnp.float32)
+            after = pltpu.roll(block, HALO, 1)
+        shifted[:, start : start + LANES] = jnp.where(low, before, after).astype(jnp.bfloat16)
+        before = after
+
     pl.semaphore_wait(barrier, expos + 1)
     for d in reversed(range(1, expos)):
 
@@ -288,6 +296,8 @@
         def _():
             template_copy(expos - d, me - d, me).start()
 
+    mine.start()
+    science_in.wait()
     for d in range(1, expos):
         science_copy(d, (me + d) % expos, me).start()
     weight_in.wait()
@@ -330,17 +340,7 @@
     for d in range(1, expos):
         template_copy(d, me, (me + expos - d) % expos).wait_recv()
 
-    block = tbuf[owner, :, LANES : LANES + span].astype(jnp.float32)
-    place = jnp.full((rows, LANES), me, jnp.int32)
-    block = jnp.concatenate(
-        [
-            jnp.where(place > 0, block[:, :LANES], 0.0),
-            block[:, LANES : span - LANES],
-            jnp.where(place < expos - 1, block[:, span - LANES :], 0.0),
-        ],
-        axis=1,
-    )
-    picked[1] = block[:, LANES - HALO : LANES - HALO + keep].astype(jnp.bfloat16)
+    picked[1] = tbuf[owner]
 
     @pl.when(tile < tiles - 1)
     def _():
@@ -569,7 +569,10 @@
         in_specs=[far] * 6,
         out_specs=(vector, vector),
         scratch_shapes=[
-            pltpu.VMEM((expos, rows, cols + 4 * LANES), jnp.bfloat16),
+            pltpu.VMEM((rows, width), jnp.bfloat16),
+            pltpu.VMEM((rows, width), jnp.bfloat16),
+            pltpu.VMEM((rows, width + 2 * HALO), jnp.bfloat16),
+            pltpu.VMEM((expos, rows, cols + 2 * HALO), jnp.bfloat16),
             pltpu.VMEM((3, rows, cols + 2 * HALO), jnp.bfloat16),
             pltpu.VMEM((expos, rows, cols), jnp.bfloat16),
             pltpu.VMEM((expos, 1, LANES), jnp.float32),
@@ -583,7 +586,7 @@
             pltpu.SMEM(orders.shape, jnp.int32),
             pltpu.SMEM(coadd_weight.shape, jnp.float32),
             pltpu.SMEM(intersection.shape, jnp.int32),
-            dma((6,)),
+            dma((8,)),
             dma((expos,)),
             dma((expos,)),
             dma((expos,)),

time: 21.7 us -> 21.1 us (0.972)
  Pallas kernels: 19.6 us -> 19 us
    pallas_call x1, Pallas kernels: 18.9 us -> 18.4 us  [window(): pl.pallas_call(functools.partial(fused, dims), out_shape=shapes, in_specs...]
where the time goes in v3:
time: 21.1 us; the launch traced here: 20.9 us
  Pallas kernels  19 us (90%)
  between operations  1.93 us (9%)
    pallas_call x1, Pallas kernels, window(): pl.pallas_call(functools.partial(fused, dims), out_shape=shapes, in_specs...  18.4 us
    pallas_call x1, Pallas kernels, window(): pl.pallas_call(store, out_shape=shapes, in_specs=[vector, vector], out_sp...  0.65 us

profile of v3, /device:TPU:0, one launch (start us, length us, event | category | flops | bytes accessed | tf_op | source)
XLA Modules:
  0.0 20.9 jit_solution(16106015505664116459)
XLA Ops:
  1.9 18.4 %shard_map.77 = (f32[1,16,1024]{2,1,0:T(8,128)S(1)}, f32[1,1,13]{2,1,0:T(1,128)S(1)}) custom-call(bf16[1,16,4096]{2,1,0:T(8,128)(2,1)} %template_ref.1, bf16[1,1,16,4096]{3,2,1,0:T(8,128)(2,1)} %science_ref.1, s32[4]{0:T(128)} %plan_ref.1, s32[2,6]{1,0:T(2,128)} %bitcast.1, f32[1,1]{1,0:T(1,128)S(6)} %copy.8.weight_ref, s32[1,1]{1,0:T(1,128)S(6)} %copy.9.inter_ref), custom_call_target="tpu_custom_call" | custom-call | tf_op jit(solution)/shard_map/pallas_call | solution.py:566
  20.3 0.7 %shard_map.78 = (f32[1,16,1024]{2,1,0:T(8,128)}, f32[1,1,13]{2,1,0:T(1,128)}) custom-call(f32[1,16,1024]{2,1,0:T(8,128)S(1)} %get-tuple-element.4.coadd_in, f32[1,1,13]{2,1,0:T(1,128)S(1)} %get-tuple-element.5.coeffs_in), custom_call_target="tpu_custom_call" | custom-call | tf_op jit(solution)/shard_map/pallas_call | solution.py:605

commit v4 on v3

--- a/solution.py
+++ b/solution.py
@@ -181,6 +181,9 @@
     keep = cols + 2 * HALO
     me = lax.axis_index("expo")
     tile = lax.axis_index("tile")
+    odd = tile % 2
+    away = (1 - odd) * ((tile + tiles - 1) // tiles)
+    near = tile + away
 
     def others():
         near = [0] + list(range(2, expos - 1))
@@ -194,6 +197,20 @@
     for d in range(1, expos):
         peer = (me + d) % expos
         pl.semaphore_signal(barrier, inc=1, device_id={"expo": peer}, device_id_type=MESH)
+    @pl.when((odd == 1) & (tile > 1))
+    def _():
+        for d in range(1, expos):
+            pl.semaphore_signal(
+                barrier,
+                inc=1,
+                device_id={"expo": (me + d) % expos, "tile": tile - 1},
+                device_id_type=MESH,
+            )
+
+    @pl.when((odd == 1) & (tile < tiles - 1))
+    def _():
+        pl.semaphore_signal(barrier, inc=1, device_id={"tile": tile + 2}, device_id_type=MESH)
+
     for d in (1, tiles - 1):
         peer = (tile + d) % tiles
         pl.semaphore_signal(barrier, inc=1, device_id={"tile": peer}, device_id_type=MESH)
@@ -218,7 +235,7 @@
     plan_in, orders_in, weight_in, inter_in, mine_science, template_in, science_in = local
     local = [template_in, science_in] + local[:5]
     mine = pltpu.make_async_copy(
-        shifted.at[:, shifted_columns(me)], tbuf.at[me], local_sem.at[7]
+        shifted.at[:, shifted_columns(me)], tbuf.at[me, 1], local_sem.at[7]
     )
     for copy in local:
         copy.start()
@@ -226,10 +243,21 @@
     def template_copy(d, target, holder):
         return pltpu.make_async_remote_copy(
             src_ref=shifted.at[:, shifted_columns(target)],
-            dst_ref=tbuf.at[holder],
+            dst_ref=tbuf.at[holder, 1 - away],
             send_sem=tsend.at[d],
-            recv_sem=trecv.at[d],
-            device_id={"expo": target},
+            recv_sem=trecv.at[1 - away, d],
+            device_id={"expo": target, "tile": near},
+            device_id_type=MESH,
+        )
+
+    def template_arrival(side, d):
+        landing = tbuf.at[(me + expos - d) % expos, side]
+        return pltpu.make_async_remote_copy(
+            src_ref=landing,
+            dst_ref=landing,
+            send_sem=tsend.at[d],
+            recv_sem=trecv.at[side, d],
+            device_id={"tile": tile - 1},
             device_id_type=MESH,
         )
 
@@ -253,14 +281,14 @@
             device_id_type=MESH,
         )
 
-    def forward_copy(side):
-        target = tile + 1 if side == 0 else tile - 1
+    def forward_copy(kind):
+        ahead, source, landing = [(-2, 0, 2), (1, 1, 0), (-1, 0, 1), (-1, 1, 2)][kind]
         return pltpu.make_async_remote_copy(
-            src_ref=picked.at[1],
-            dst_ref=picked.at[2 * side],
-            send_sem=fsend.at[side],
-            recv_sem=frecv.at[side],
-            device_id={"tile": target},
+            src_ref=picked.at[source],
+            dst_ref=picked.at[landing],
+            send_sem=fsend.at[kind],
+            recv_sem=frecv.at[kind],
+            device_id={"tile": tile + ahead},
             device_id_type=MESH,
         )
 
@@ -285,18 +313,29 @@
         shifted[:, start : start + LANES] = jnp.where(low, before, after).astype(jnp.bfloat16)
         before = after
 
-    pl.semaphore_wait(barrier, expos + 1)
+    @pl.when(away == 1)
+    def _():
+        pl.semaphore_wait(barrier, 2 * expos)
+
+    @pl.when(tile < 2)
+    def _():
+        pl.semaphore_wait(barrier, expos + 1)
+
+    @pl.when((odd == 1) & (tile > 1))
+    def _():
+        pl.semaphore_wait(barrier, expos + 2)
+
     for d in reversed(range(1, expos)):
-
-        @pl.when(me + d < expos)
-        def _():
-            template_copy(d, me + d, me).start()
-
-        @pl.when(me - d >= 0)
-        def _():
-            template_copy(expos - d, me - d, me).start()
-
-    mine.start()
+        template_copy(d, (me + d) % expos, me).start()
+
+    @pl.when(away == 1)
+    def _():
+        template_copy(0, me, me).start()
+
+    @pl.when(away == 0)
+    def _():
+        mine.start()
+
     science_in.wait()
     for d in range(1, expos):
         science_copy(d, (me + d) % expos, me).start()
@@ -336,25 +375,46 @@
 
     plan_in.wait()
     owner = plan_mem[0]
-    mine.wait()
-    for d in range(1, expos):
-        template_copy(d, me, (me + expos - d) % expos).wait_recv()
-
-    picked[1] = tbuf[owner]
-
-    @pl.when(tile < tiles - 1)
-    def _():
+
+    @pl.when(away == 0)
+    def _():
+        mine.wait()
+        for d in range(1, expos):
+            template_arrival(1, d).wait_recv()
+
+    @pl.when((odd == 1) & (tile > 1))
+    def _():
+        for d in range(expos):
+            template_arrival(0, d).wait_recv()
+        picked[0] = tbuf[owner, 0]
         forward_copy(0).start()
-
-    @pl.when(tile > 0)
-    def _():
-        forward_copy(1).start()
-
-    @pl.when(tile > 0)
+        forward_copy(2).start()
+
+    @pl.when(away == 0)
+    def _():
+        picked[1] = tbuf[owner, 1]
+
+        @pl.when(tile < tiles - 1)
+        def _():
+            forward_copy(1).start()
+
+        @pl.when(tile > 0)
+        def _():
+            forward_copy(3).start()
+
+    @pl.when((odd == 1) & (tile < tiles - 1))
     def _():
         forward_copy(0).wait_recv()
 
-    @pl.when(tile < tiles - 1)
+    @pl.when(away == 1)
+    def _():
+        forward_copy(2).wait_recv()
+
+    @pl.when(odd == 0)
+    def _():
+        forward_copy(3).wait_recv()
+
+    @pl.when((away == 1) | (tile == 1))
     def _():
         forward_copy(1).wait_recv()
 
@@ -411,19 +471,22 @@
         fold_ref[3 * len(PAIRS) + u] = sums[0]
         fold_ref[3 * len(PAIRS) + NB + u] = once(sums)
 
-    mine_science.wait()
-    for d in range(1, expos):
-        science_copy(d, me, (me + expos - d) % expos).wait_recv()
-    for e in range(expos):
+    used = count + NU * expos
+    for index in range(used, LANES):
+        fold_ref[index] = jnp.zeros((8, LANES), jnp.float32)
+
+    for d in range(expos):
+        e = (me + expos - d) % expos
+        if d == 0:
+            mine_science.wait()
+        else:
+            science_copy(d, me, e).wait_recv()
         science = [science_at(e, b) for b in range(per)]
         for u in range(NB):
             sums = running(lambda b: fold(conv_at(u, b) * science[b]), 2)
             fold_ref[count + u * expos + e] = sums[0]
             fold_ref[count + (NB + u) * expos + e] = once(sums)
         fold_ref[count + 2 * NB * expos + e] = running(lambda b: fold(science[b]), 1)[0]
-    used = count + NU * expos
-    for index in range(used, LANES):
-        fold_ref[index] = jnp.zeros((8, LANES), jnp.float32)
 
     packed = jnp.concatenate(
         [sublane_sums([fold_ref[g + s] for s in range(8)]) for g in range(0, LANES, 8)], axis=0
@@ -513,13 +576,24 @@
         science_copy(d, (me + d) % expos, me).wait_send()
         weight_copy(d, (me + d) % expos, me).wait_send()
 
-    @pl.when(tile < tiles - 1)
+    @pl.when(away == 1)
+    def _():
+        template_copy(0, me, me).wait_send()
+
+    @pl.when((odd == 1) & (tile > 1))
     def _():
         forward_copy(0).wait_send()
-
-    @pl.when(tile > 0)
-    def _():
-        forward_copy(1).wait_send()
+        forward_copy(2).wait_send()
+
+    @pl.when(away == 0)
+    def _():
+        @pl.when(tile < tiles - 1)
+        def _():
+            forward_copy(1).wait_send()
+
+        @pl.when(tile > 0)
+        def _():
+            forward_copy(3).wait_send()
 
     for index, e, t in others():
         stat_copy(index, me, tile, e, t).wait_send()
@@ -545,6 +619,7 @@
         and template.shape[0] == 1
         and expos > 2
         and tiles > 2
+        and tiles == 4
         and width % expos == 0
         and cols % LANES == 0
         and cols // LANES > 2
@@ -572,7 +647,7 @@
             pltpu.VMEM((rows, width), jnp.bfloat16),
             pltpu.VMEM((rows, width), jnp.bfloat16),
             pltpu.VMEM((rows, width + 2 * HALO), jnp.bfloat16),
-            pltpu.VMEM((expos, rows, cols + 2 * HALO), jnp.bfloat16),
+            pltpu.VMEM((expos, 2, rows, cols + 2 * HALO), jnp.bfloat16),
             pltpu.VMEM((3, rows, cols + 2 * HALO), jnp.bfloat16),
             pltpu.VMEM((expos, rows, cols), jnp.bfloat16),
             pltpu.VMEM((expos, 1, LANES), jnp.float32),
@@ -588,13 +663,13 @@
             pltpu.SMEM(intersection.shape, jnp.int32),
             dma((8,)),
             dma((expos,)),
+            dma((2, expos)),
             dma((expos,)),
             dma((expos,)),
             dma((expos,)),
             dma((expos,)),
-            dma((expos,)),
-            dma((2,)),
-            dma((2,)),
+            dma((4,)),
+            dma((4,)),
             dma((expos * tiles,)),
             dma((expos * tiles,)),
         ],

time: 21.1 us -> 21.1 us (level)
  no operation moved by 1% of the time
where the time goes in v4:
time: 21.1 us; the launch traced here: 20.9 us
  Pallas kernels  19 us (90%)
  between operations  1.93 us (9%)
    pallas_call x1, Pallas kernels, window(): pl.pallas_call(functools.partial(fused, dims), out_shape=shapes, in_specs...  18.4 us
    pallas_call x1, Pallas kernels, window(): pl.pallas_call(store, out_shape=shapes, in_specs=[vector, vector], out_sp...  0.65 us

profile of v4, /device:TPU:0, one launch (start us, length us, event | category | flops | bytes accessed | tf_op | source)
XLA Modules:
  0.0 20.9 jit_solution(9251427234411774637)
XLA Ops:
  1.9 18.4 %shard_map.77 = (f32[1,16,1024]{2,1,0:T(8,128)S(1)}, f32[1,1,13]{2,1,0:T(1,128)S(1)}) custom-call(bf16[1,16,4096]{2,1,0:T(8,128)(2,1)} %template_ref.1, bf16[1,1,16,4096]{3,2,1,0:T(8,128)(2,1)} %science_ref.1, s32[4]{0:T(128)} %plan_ref.1, s32[2,6]{1,0:T(2,128)} %bitcast.1, f32[1,1]{1,0:T(1,128)S(6)} %copy.8.weight_ref, s32[1,1]{1,0:T(1,128)S(6)} %copy.9.inter_ref), custom_call_target="tpu_custom_call" | custom-call | tf_op jit(solution)/shard_map/pallas_call | solution.py:641
  20.3 0.7 %shard_map.78 = (f32[1,16,1024]{2,1,0:T(8,128)}, f32[1,1,13]{2,1,0:T(1,128)}) custom-call(f32[1,16,1024]{2,1,0:T(8,128)S(1)} %get-tuple-element.4.coadd_in, f32[1,1,13]{2,1,0:T(1,128)S(1)} %get-tuple-element.5.coeffs_in), custom_call_target="tpu_custom_call" | custom-call | tf_op jit(solution)/shard_map/pallas_call | solution.py:680

commit v5 on v3

--- a/solution.py
+++ b/solution.py
@@ -411,19 +411,22 @@
         fold_ref[3 * len(PAIRS) + u] = sums[0]
         fold_ref[3 * len(PAIRS) + NB + u] = once(sums)
 
-    mine_science.wait()
-    for d in range(1, expos):
-        science_copy(d, me, (me + expos - d) % expos).wait_recv()
-    for e in range(expos):
+    used = count + NU * expos
+    for index in range(used, LANES):
+        fold_ref[index] = jnp.zeros((8, LANES), jnp.float32)
+
+    for d in range(expos):
+        e = (me + expos - d) % expos
+        if d == 0:
+            mine_science.wait()
+        else:
+            science_copy(d, me, e).wait_recv()
         science = [science_at(e, b) for b in range(per)]
         for u in range(NB):
             sums = running(lambda b: fold(conv_at(u, b) * science[b]), 2)
             fold_ref[count + u * expos + e] = sums[0]
             fold_ref[count + (NB + u) * expos + e] = once(sums)
         fold_ref[count + 2 * NB * expos + e] = running(lambda b: fold(science[b]), 1)[0]
-    used = count + NU * expos
-    for index in range(used, LANES):
-        fold_ref[index] = jnp.zeros((8, LANES), jnp.float32)
 
     packed = jnp.concatenate(
         [sublane_sums([fold_ref[g + s] for s in range(8)]) for g in range(0, LANES, 8)], axis=0

time: 21.1 us -> 21.1 us (level)
  no operation moved by 1% of the time
where the time goes in v5:
time: 21.1 us; the launch traced here: 20.9 us
  Pallas kernels  19 us (90%)
  between operations  1.93 us (9%)
    pallas_call x1, Pallas kernels, window(): pl.pallas_call(functools.partial(fused, dims), out_shape=shapes, in_specs...  18.4 us
    pallas_call x1, Pallas kernels, window(): pl.pallas_call(store, out_shape=shapes, in_specs=[vector, vector], out_sp...  0.65 us

profile of v5, /device:TPU:0, one launch (start us, length us, event | category | flops | bytes accessed | tf_op | source)
XLA Modules:
  0.0 20.9 jit_solution(1466982788032673820)
XLA Ops:
  1.9 18.4 %shard_map.77 = (f32[1,16,1024]{2,1,0:T(8,128)S(1)}, f32[1,1,13]{2,1,0:T(1,128)S(1)}) custom-call(bf16[1,16,4096]{2,1,0:T(8,128)(2,1)} %template_ref.1, bf16[1,1,16,4096]{3,2,1,0:T(8,128)(2,1)} %science_ref.1, s32[4]{0:T(128)} %plan_ref.1, s32[2,6]{1,0:T(2,128)} %bitcast.1, f32[1,1]{1,0:T(1,128)S(6)} %copy.8.weight_ref, s32[1,1]{1,0:T(1,128)S(6)} %copy.9.inter_ref), custom_call_target="tpu_custom_call" | custom-call | tf_op jit(solution)/shard_map/pallas_call | solution.py:569
  20.3 0.7 %shard_map.78 = (f32[1,16,1024]{2,1,0:T(8,128)}, f32[1,1,13]{2,1,0:T(1,128)}) custom-call(f32[1,16,1024]{2,1,0:T(8,128)S(1)} %get-tuple-element.4.coadd_in, f32[1,1,13]{2,1,0:T(1,128)S(1)} %get-tuple-element.5.coeffs_in), custom_call_target="tpu_custom_call" | custom-call | tf_op jit(solution)/shard_map/pallas_call | solution.py:608
